TPU v7x, 256 devices: a whole 4x4x8 slice. The times are simulated.
256 devices in a mesh: walk: 16 (over z, x_hi), blk: 16 (over x_lo, y, core).
Axes of the slice: x: 4 (x_hi: 2, x_lo: 2; x = x_hi * 2 + x_lo), y: 4, z: 8, core: 2. Of those that a mesh axis runs over, the one named last changes fastest.
Arguments:
- vertex_times: int32 [16, 1024], P('blk'), may hold values from 0 to 4095
- vertex_sites: int32 [16, 1024], P('blk'), may hold values from 0 to 15
- vertex_matrix: bfloat16 [16, 1024, 1024], P('blk', 'walk'), may hold values from -0.1875 to 0.1875
- bare_green: float32 [2, 1024], replicated, may hold values from -3 to 3
- transfer_momentum: int32 [16], replicated, may hold values from 0 to 15, each once
- transfers: int32 [32], replicated, may hold values from 0 to 31, each once
Outputs:
- g4: float32 [2, 32, 1024, 1024], P(None, 'blk', 'walk')
Inputs may be any that keep to these rules, and one draw needn't show every extreme that they name: `transfer_momentum`: each of 0 to 15 appears exactly once. `transfers`: each of 0 to 31 appears exactly once.
All inputs are finite; a program needn't handle non-finite values.
Results may differ from a plain program's by a relative error of at most 0.0071.
Values may be sent and summed in bfloat16 or wider, within the bound.
A program may use at most 64 MiB of HBM per device.

v0:
```python
import math
import jax
import jax.numpy as jnp
from jax import lax
from jax.sharding import PartitionSpec as P

NM = 16
NF = 64
NV = 1024
NT = 4096
QB = 2
side_length = 4


def fourier_table(times, sites):
    points = jnp.arange(NM * NF, dtype=jnp.int32)
    momentum = points // NF
    frequency = points % NF
    momentum_x = momentum // side_length
    momentum_y = momentum % side_length
    site_x = sites // side_length
    site_y = sites % side_length
    odd_part = 4 * (2 * frequency + 1 - NF)
    phase = odd_part[:, None] * times[None, :] - 2 * NT * (
        momentum_x[:, None] * site_x[None, :] + momentum_y[:, None] * site_y[None, :]
    )
    phase = jnp.mod(phase, 8 * NT)
    angle = phase.astype(jnp.float32) * (2.0 * math.pi / (8 * NT))
    return (jnp.cos(angle).astype(jnp.bfloat16), jnp.sin(angle).astype(jnp.bfloat16))


def assemble(spread_re, spread_im, row_re, row_im, col_re, col_im, rows, cols):
    scale = NV ** (-0.5)
    part_re = (spread_re * col_re[None, :] - spread_im * col_im[None, :]) * scale
    part_im = (spread_re * col_im[None, :] + spread_im * col_re[None, :]) * scale
    diagonal = (rows[:, None] == cols[None, :]).astype(jnp.float32)
    green_re = row_re[:, None] * (part_re + diagonal) - row_im[:, None] * part_im
    green_im = row_re[:, None] * part_im + row_im[:, None] * (part_re + diagonal)
    return (green_re.astype(jnp.bfloat16), green_im.astype(jnp.bfloat16))


def send_layout(panels, shift):
    count = panels.shape[0]
    row_count = panels.shape[2]
    grid = panels.reshape(count, 2, row_count, NM, NF)
    grid = jnp.take(grid, shift, axis=3)
    grid = jnp.transpose(grid, (0, 1, 3, 2, 4))
    return grid.reshape(count, 2, 1, NM, row_count * NF)


def receive_layout(incoming, shift):
    count, _, groups, moments, flat = incoming.shape
    row_count = flat // NF
    grid = incoming.reshape(count, 2, groups, moments, row_count, NF)
    grid = jnp.transpose(grid, (0, 1, 3, 5, 2, 4))
    grid = jnp.take(grid, shift, axis=4)
    return grid.reshape(count, 2, moments * NF, NM * NF)


def accumulate(total, direct, turned, offsets):
    moments = turned.shape[1] // NF
    grid = turned.reshape(2, moments, NF, NM, NF)
    near = direct.astype(jnp.float32)
    spots = jnp.arange(NF, dtype=jnp.int32)
    for position in range(offsets.shape[0]):
        offset = offsets[position]
        rolled = jnp.roll(grid, -offset, axis=2)
        rolled = jnp.roll(rolled, -offset, axis=4)
        valid = (spots + offset >= 0) & (spots + offset < NF)
        keep = valid[:, None, None] & valid[None, None, :]
        masked = jnp.where(keep[None, None], rolled, jnp.zeros((), rolled.dtype))
        shifted = masked.reshape(2, moments * NF, NM * NF).astype(jnp.float32)
        part_re = near[0] * shifted[0] - near[1] * shifted[1]
        part_im = near[0] * shifted[1] + near[1] * shifted[0]
        total = total.at[:, position].add(jnp.stack([part_re, part_im]))
    return total


def walker_sum(total, direct_panels, turned_panels, offsets):

    def step(carry, pair):
        return (accumulate(carry, pair[0], pair[1], offsets), None)

    result, _ = lax.scan(step, total, (direct_panels, turned_panels))
    return result


def shards(vertex_times, vertex_sites, vertex_matrix, bare_green, transfer_momentum, transfers):
    walk_count = lax.axis_size("walk")
    walk_index = lax.axis_index("walk")
    blk_index = lax.axis_index("blk")
    points = NM * NF
    row_count = points // walk_count
    four_re, four_im = fourier_table(vertex_times[0], vertex_sites[0])
    row_start = walk_index * row_count
    rows_re = lax.dynamic_slice_in_dim(four_re, row_start, row_count, 0)
    rows_im = lax.dynamic_slice_in_dim(four_im, row_start, row_count, 0)
    piece = lax.all_gather(vertex_matrix[0], "walk", axis=0, tiled=True)
    inner_re = jnp.dot(rows_re, piece, preferred_element_type=jnp.float32)
    inner_im = jnp.dot(rows_im, piece, preferred_element_type=jnp.float32)
    inner_re = inner_re.astype(jnp.bfloat16)
    inner_im = inner_im.astype(jnp.bfloat16)
    contract = (((1,), (1,)), ((), ()))

    def product(left, right):
        return lax.dot_general(left, right, contract, preferred_element_type=jnp.float32)

    spread_re = product(inner_re, four_re) + product(inner_im, four_im)
    spread_im = product(inner_im, four_re) - product(inner_re, four_im)
    rows = row_start + jnp.arange(row_count, dtype=jnp.int32)
    cols = jnp.arange(points, dtype=jnp.int32)
    row_re = lax.dynamic_slice_in_dim(bare_green[0], row_start, row_count)
    row_im = lax.dynamic_slice_in_dim(bare_green[1], row_start, row_count)
    green_re, green_im = assemble(
        spread_re, spread_im, row_re, row_im, bare_green[0], bare_green[1], rows, cols
    )
    direct = jnp.stack([green_re, green_im])
    window_size = transfers.shape[0]
    offsets = lax.dynamic_slice_in_dim(transfers, blk_index * QB, QB) - window_size // 2
    slab = jnp.zeros((2, QB, row_count, points), jnp.float32)
    outgoing = send_layout(direct[None], transfer_momentum)
    incoming = lax.all_to_all(outgoing, "walk", split_axis=3, concat_axis=2, tiled=True)
    turned = receive_layout(incoming, transfer_momentum)
    return walker_sum(
        slab,
        lax.all_gather(direct[None], "blk", axis=0, tiled=True),
        lax.all_gather(turned, "blk", axis=0, tiled=True),
        offsets,
    )


def solution(mesh):
    return jax.shard_map(
        shards,
        mesh=mesh,
        in_specs=(P("blk", None), P("blk", None), P("blk", "walk", None), P(), P(), P()),
        out_specs=P(None, "blk", "walk", None),
        check_vma=False,
    )
```

profile of v0, /device:TPU:1, one launch (start us, length us, event | category | flops | bytes accessed | tf_op | source)
XLA Modules:
  0.0 327.5 jit_solution(9244534965251903392)
XLA Ops:
  8.9 20.5 %cosine_convert_fusion = (bf16[1024,1024]{1,0:T(8,128)(2,1)S(1)}, bf16[1024,1024]{1,0:T(8,128)(2,1)}) fusion(s32[1024]{0:T(1024)S(1)} %bitcast.120, s32[1024]{0:T(1024)S(1)} %get-tuple-element.158, s32[1024]{0:T(1024)S(1)} %bitcast.117, s32[1024]{0:T(1024)S(1)} %get-tuple-element.159, s32[1024]{0:T(1024)} %bitcast.125, s32[1024]{0:T(1024)S(1)} %fusion.25), kind=kLoop, calls=%fused_computation.38 | loop fusion | flops 22020096 | bytes 4218880 | tf_op jit(solution)/shard_map/convert_element_type | solution.py:29
  29.4 66.0 %all-gather.8.cloned.1.call-done = bf16[1,1024,1024]{2,1,0:T(8,128)(2,1)} async-done(((bf16[1,64,1024]{2,1,0:T(8,128)(2,1)}), bf16[1,1024,1024]{2,1,0:T(8,128)(2,1)}) %all-gather.8.cloned.1.call-update) | async-done | bytes 2097168 | tf_op jit(solution)/shard_map/all_gather | solution.py:98
  95.4 2.2 fusion.14
  98.5 1.4 fusion.17
  100.6 16.4 %convolution_add_fusion = f32[64,1024]{1,0:T(8,128)S(1)} fusion(f32[64,1024]{1,0:T(8,128)S(1)} %fusion.47, bf16[64,1024]{1,0:T(8,128)(2,1)S(1)} %fusion.17, s32[1024]{0:T(1024)S(1)} %bitcast.121, s32[1024]{0:T(1024)S(1)} %get-tuple-element.158, s32[1024]{0:T(1024)S(1)} %bitcast.118, s32[1024]{0:T(1024)S(1)} %get-tuple-element.159, s32[1024]{0:T(1024)S(1)} %bitcast.126, ...), kind=kOutput, calls=%fused_computation.44 | convolution fusion | flops 155254784 | bytes 679936 | tf_op jit(solution)/shard_map/dot_general | solution.py:106
  117.1 16.6 %subtract_convert_fusion = (bf16[64,1024]{1,0:T(8,128)(2,1)S(1)}, bf16[64,1024]{1,0:T(8,128)(2,1)S(1)}) fusion(f32[64]{0:T(128)S(1)} %get-tuple-element.156, f32[64]{0:T(128)S(1)} %get-tuple-element.129, f32[1024]{0:T(1024)S(1)} %bitcast.123, f32[64,1024]{1,0:T(8,128)S(1)} %convolution_add_fusion, f32[1024]{0:T(1024)S(1)} %bitcast.124, ...), kind=kOutput, calls=%fused_computation.52 | convolution fusion | flops 156434432 | bytes 951552 | tf_op jit(solution)/shard_map/dot_general | solution.py:106
  137.3 4.0 %all-to-all-start = ((bf16[1,2,1,16,4096]{4,1,2,0,3:T(2,128)(2,1)}), bf16[1,2,1,16,4096]{4,1,2,0,3:T(2,128)(2,1)S(1)}, u32[]{:S(2)}, u32[]{:S(2)}) async-start(bf16[1,2,1,16,4096]{4,1,2,0,3:T(2,128)(2,1)} %bitcast.28), calls=%async_computation | async-start | bytes 524288 | tf_op jit(solution)/shard_map/all_to_all | solution.py:122
  141.5 11.0 %all-to-all-done = bf16[1,2,1,16,4096]{4,1,2,0,3:T(2,128)(2,1)S(1)} async-done(((bf16[1,2,1,16,4096]{4,1,2,0,3:T(2,128)(2,1)}), bf16[1,2,1,16,4096]{4,1,2,0,3:T(2,128)(2,1)S(1)}, u32[]{:S(2)}, u32[]{:S(2)}) %all-to-all-start) | async-done | bytes 262176 | tf_op jit(solution)/shard_map/all_to_all | solution.py:122
  157.3 18.6 %all-gather.10.cloned.1.call-done = bf16[32,64,1024]{2,1,0:T(8,128)(2,1)} async-done(((bf16[2,64,1024]{2,1,0:T(8,128)(2,1)}), bf16[32,64,1024]{2,1,0:T(8,128)(2,1)}) %all-gather.10.cloned.1.call-update) | async-done | bytes 4194320 | tf_op jit(solution)/shard_map/all_gather | solution.py:126
  175.9 41.9 %all-gather.6.cloned.1.call-done = bf16[16,2,64,1024]{3,2,1,0:T(8,128)(2,1)} async-done(((bf16[1,2,64,1024]{3,2,1,0:T(8,128)(2,1)}), bf16[16,2,64,1024]{3,2,1,0:T(8,128)(2,1)}) %all-gather.6.cloned.1.call-update) | async-done | bytes 4194320 | tf_op jit(solution)/shard_map/all_gather | solution.py:127
  218.0 101.8 %while.14 = (s32[]{:T(128)}, f32[2,2,64,1024]{3,2,1,0:T(8,128)S(1)}, bf16[16,2,64,1024]{3,2,1,0:T(8,128)(2,1)}, s32[2]{0:T(128)S(1)}, bf16[16,2,64,1024]{3,2,1,0...) while((s32[]{:T(128)}, ...), condition=%wide.region_1.4_spmd, body=%wide.region_0.3_spmd.sunk | while | flops 3023392 | bytes 18367192 | solution.py:84
  220.4 1.2 compare_and_fusion.4
  226.7 1.2 compare_and_fusion.4
  233.1 1.2 compare_and_fusion.4
  239.5 1.2 compare_and_fusion.4
  245.8 1.2 compare_and_fusion.4
  252.2 1.2 compare_and_fusion.4
  258.5 1.2 compare_and_fusion.4
  264.9 1.2 compare_and_fusion.4
  271.3 1.2 compare_and_fusion.4
  277.6 1.2 compare_and_fusion.4
  284.0 1.2 compare_and_fusion.4
  290.4 1.2 compare_and_fusion.4
  309.5 1.2 compare_and_fusion.4
  (371 shorter events, 95.7 us)
Async XLA Ops:
  6.5 88.9 %all-gather.8.cloned.1.call-start = ((), (), s32[]{:S(2)}) async-start(), calls=%async_computation.2 | async-start | bytes 2228224 | tf_op jit(solution)/shard_map/all_gather | solution.py:98
  7.3 168.7 %all-gather.10.cloned.1.call-start = ((), (), s32[]{:S(2)}) async-start(), calls=%async_computation.3 | async-start | bytes 4456448 | tf_op jit(solution)/shard_map/all_gather | solution.py:126
  95.4 3.0 copy-start.1
  97.7 2.9 copy-start.2
  117.0 17.4 %copy-start.3 = (s32[16]{0:T(128)S(1)}, s32[16]{0:T(128)}, u32[]{:S(2)}) copy-start(s32[16]{0:T(128)} %param.20) | copy-start | bytes 196
  136.0 19.3 %copy-start.4 = (s32[32]{0:T(128)S(1)}, s32[32]{0:T(128)}, u32[]{:S(2)}) copy-start(s32[32]{0:T(128)} %param.21) | copy-start | bytes 388
  137.3 15.2 %all-to-all-start = ((bf16[1,2,1,16,4096]{4,1,2,0,3:T(2,128)(2,1)}), bf16[1,2,1,16,4096]{4,1,2,0,3:T(2,128)(2,1)S(1)}, u32[]{:S(2)}, u32[]{:S(2)}) async-start(bf16[1,2,1,16,4096]{4,1,2,0,3:T(2,128)(2,1)} %bitcast.28), calls=%async_computation | async-start | bytes 524288 | tf_op jit(solution)/shard_map/all_to_all | solution.py:122
  141.3 76.5 %all-gather.6.cloned.1.call-start = ((), (), s32[]{:S(2)}) async-start(), calls=%async_computation.1 | async-start | bytes 4456448 | tf_op jit(solution)/shard_map/all_gather | solution.py:127
  319.8 1.0 copy-start
Sparse Core Ops, SparseCore 0:
  9.9 85.4 all-gather.7
  134.5 41.3 all-gather.9
  177.8 40.0 all-gather.5
where the time goes:
time: 331 us; the launch traced here: 328 us
  waiting for transfers between devices  138 us (42%)
  other arithmetic  88.1 us (27%)
  local copies, waits for them, and re-layouts  41.2 us (12%)
  matrix products  38.1 us (12%)
  between operations  14.9 us (5%)
  starting transfers between devices  4.11 us (1%)
    all_gather x1, waiting for transfers between devices, shards(): piece = lax.all_gather(vertex_matrix[0], 'walk', axis=0, tiled=True)  66 us
    all_gather x1, waiting for transfers between devices, shards(): lax.all_gather(turned, 'blk', axis=0, tiled=True)  41.9 us
    dot_general x4, matrix products, product(): lax.dot_general(left, right, contract, preferred_element_type=jnp.float32)  34.5 us
    convert_element_type x1, other arithmetic, fourier_table(): jnp.cos(angle).astype(jnp.bfloat16)  20.5 us
    convert_element_type x32, other arithmetic, accumulate(): shifted = masked.reshape(2, moments * NF, NM * NF).astype(jnp.float32)  19.8 us
    and x16, other arithmetic, accumulate(): valid = (spots + offset >= 0) & (spots + offset < NF)  19.1 us
    all_gather x1, waiting for transfers between devices, shards(): lax.all_gather(direct[None], 'blk', axis=0, tiled=True)  18.6 us
    convert_element_type x16, other arithmetic, accumulate(): near = direct.astype(jnp.float32)  17.6 us
  transfers between devices with their start and end apart: 4, of which 4 were waited for; matrix products, arithmetic and copies ran while one was open for 9% of the time, Pallas kernels for 0%

commit v1 on v0

--- a/solution.py
+++ b/solution.py
@@ -95,7 +95,9 @@
     row_start = walk_index * row_count
     rows_re = lax.dynamic_slice_in_dim(four_re, row_start, row_count, 0)
     rows_im = lax.dynamic_slice_in_dim(four_im, row_start, row_count, 0)
-    piece = lax.all_gather(vertex_matrix[0], "walk", axis=0, tiled=True)
+    piece = jnp.concatenate(
+        lax.all_to_all(jnp.stack([vertex_matrix[0]] * lax.axis_size("walk")), "walk", 0, 0), axis=0
+    )
     inner_re = jnp.dot(rows_re, piece, preferred_element_type=jnp.float32)
     inner_im = jnp.dot(rows_im, piece, preferred_element_type=jnp.float32)
     inner_re = inner_re.astype(jnp.bfloat16)

time: 331 us -> 306 us (0.924)
  waiting for transfers between devices: 138 us -> 98.4 us
  starting transfers between devices: 4.11 us -> 17.4 us
    all_gather x1 -> x0, waiting for transfers between devices: 66 us -> none  [shards(): piece = lax.all_gather(vertex_matrix[0], 'walk', axis=0, tiled=True)]
    all_to_all x0 -> x1, waiting for transfers between devices: none -> 30 us  [shards(): lax.all_to_all(jnp.stack([vertex_matrix[0]] * lax.axis_size('walk')), 'wa...]
    all_to_all x0 -> x1, starting transfers between devices: none -> 11.6 us  [shards(): lax.all_to_all(jnp.stack([vertex_matrix[0]] * lax.axis_size('walk')), 'wa...]
    all_gather x1, waiting for transfers between devices: 18.6 us -> 14.3 us  [shards(): lax.all_gather(direct[None], 'blk', axis=0, tiled=True)]
where the time goes in v1:
time: 306 us; the launch traced here: 302 us
  waiting for transfers between devices  98.4 us (32%)
  other arithmetic  86.7 us (28%)
  local copies, waits for them, and re-layouts  43 us (14%)
  matrix products  38.7 us (13%)
  starting transfers between devices  17.4 us (6%)
  between operations  15.2 us (5%)
    all_gather x1, waiting for transfers between devices, shards(): lax.all_gather(turned, 'blk', axis=0, tiled=True)  42.1 us
    dot_general x4, matrix products, product(): lax.dot_general(left, right, contract, preferred_element_type=jnp.float32)  34.5 us
    all_to_all x1, waiting for transfers between devices, shards(): lax.all_to_all(jnp.stack([vertex_matrix[0]] * lax.axis_size('walk')), 'wa...  30 us
    convert_element_type x32, other arithmetic, accumulate(): shifted = masked.reshape(2, moments * NF, NM * NF).astype(jnp.float32)  19.8 us
    convert_element_type x1, other arithmetic, fourier_table(): jnp.cos(angle).astype(jnp.bfloat16)  19.8 us
    and x16, other arithmetic, accumulate(): valid = (spots + offset >= 0) & (spots + offset < NF)  19.1 us
    convert_element_type x16, other arithmetic, accumulate(): near = direct.astype(jnp.float32)  17.6 us
    all_gather x1, waiting for transfers between devices, shards(): lax.all_gather(direct[None], 'blk', axis=0, tiled=True)  14.3 us
  transfers between devices with their start and end apart: 4, of which 4 were waited for; matrix products, arithmetic and copies ran while one was open for 9% of the time, Pallas kernels for 0%

profile of v1, /device:TPU:1, one launch (start us, length us, event | category | flops | bytes accessed | tf_op | source)
XLA Modules:
  0.0 302.2 jit_solution(17308348800461946594)
XLA Ops:
  6.5 2.5 stack.34
  9.0 11.6 %all-to-all-start = ((bf16[16,64,1024]{2,1,0:T(8,128)(2,1)}), bf16[16,64,1024]{2,1,0:T(8,128)(2,1)}, u32[]{:S(2)}, u32[]{:S(2)}) async-start(bf16[16,64,1024]{2,1,0:T(8,128)(2,1)} %stack.34), calls=%async_computation | async-start | bytes 4194304 | tf_op jit(solution)/shard_map/all_to_all | solution.py:99
  20.9 19.8 %cosine_convert_fusion = (bf16[1024,1024]{1,0:T(8,128)(2,1)S(1)}, bf16[1024,1024]{1,0:T(8,128)(2,1)}) fusion(s32[1024]{0:T(1024)S(1)} %bitcast.116, s32[1024]{0:T(1024)S(1)} %get-tuple-element.158, s32[1024]{0:T(1024)S(1)} %bitcast.113, s32[1024]{0:T(1024)S(1)} %get-tuple-element.159, s32[1024]{0:T(1024)S(1)} %bitcast.121, s32[1024]{0:T(1024)S(1)} %fusion.15), kind=kLoop, calls=%fused_computation.38 | loop fusion | flops 22020096 | bytes 4218880 | tf_op jit(solution)/shard_map/convert_element_type | solution.py:29
  40.7 30.0 %all-to-all-done = bf16[16,64,1024]{2,1,0:T(8,128)(2,1)} async-done(((bf16[16,64,1024]{2,1,0:T(8,128)(2,1)}), bf16[16,64,1024]{2,1,0:T(8,128)(2,1)}, u32[]{:S(2)}, u32[]{:S(2)}) %all-to-all-start) | async-done | bytes 2097184 | tf_op jit(solution)/shard_map/all_to_all | solution.py:99
  70.7 2.1 convolution_convert_fusion.1
  73.5 2.2 convolution_convert_fusion
  76.4 16.4 %convolution_add_fusion = f32[64,1024]{1,0:T(8,128)S(1)} fusion(f32[64,1024]{1,0:T(8,128)S(1)} %fusion.37, bf16[64,1024]{1,0:T(8,128)(2,1)S(1)} %convolution_convert_fusion, s32[1024]{0:T(1024)S(1)} %bitcast.117, s32[1024]{0:T(1024)S(1)} %get-tuple-element.158, s32[1024]{0:T(1024)S(1)} %bitcast.114, s32[1024]{0:T(1024)S(1)} %get-tuple-element.159, ...), kind=kOutput, calls=%fused_computation.40 | convolution fusion | flops 155254784 | bytes 679936 | tf_op jit(solution)/shard_map/dot_general | solution.py:108
  92.9 16.6 %subtract_convert_fusion = (bf16[64,1024]{1,0:T(8,128)(2,1)S(1)}, bf16[64,1024]{1,0:T(8,128)(2,1)S(1)}) fusion(f32[64]{0:T(128)S(1)} %get-tuple-element.156, f32[64]{0:T(128)S(1)} %get-tuple-element.129, f32[1024]{0:T(1024)S(1)} %bitcast.119, f32[64,1024]{1,0:T(8,128)S(1)} %convolution_add_fusion, f32[1024]{0:T(1024)S(1)} %bitcast.120, ...), kind=kOutput, calls=%fused_computation.48 | convolution fusion | flops 156434432 | bytes 951552 | tf_op jit(solution)/shard_map/dot_general | solution.py:108
  113.1 5.7 %all-to-all-start.1 = ((bf16[1,2,1,16,4096]{4,1,2,0,3:T(2,128)(2,1)}), bf16[1,2,1,16,4096]{4,1,2,0,3:T(2,128)(2,1)S(1)}, u32[]{:S(2)}, u32[]{:S(2)}) async-start(bf16[1,2,1,16,4096]{4,1,2,0,3:T(2,128)(2,1)} %bitcast.29), calls=%async_computation.1 | async-start | bytes 524288 | tf_op jit(solution)/shard_map/all_to_all | solution.py:124
  119.0 12.0 %all-to-all-done.1 = bf16[1,2,1,16,4096]{4,1,2,0,3:T(2,128)(2,1)S(1)} async-done(((bf16[1,2,1,16,4096]{4,1,2,0,3:T(2,128)(2,1)}), bf16[1,2,1,16,4096]{4,1,2,0,3:T(2,128)(2,1)S(1)}, u32[]{:S(2)}, u32[]{:S(2)}) %all-to-all-start.1) | async-done | bytes 262176 | tf_op jit(solution)/shard_map/all_to_all | solution.py:124
  135.8 14.3 %all-gather.6.cloned.1.call-done = bf16[32,64,1024]{2,1,0:T(8,128)(2,1)} async-done(((bf16[2,64,1024]{2,1,0:T(8,128)(2,1)}), bf16[32,64,1024]{2,1,0:T(8,128)(2,1)}) %all-gather.6.cloned.1.call-update) | async-done | bytes 4194320 | tf_op jit(solution)/shard_map/all_gather | solution.py:128
  150.0 42.1 %all-gather.4.cloned.1.call-done = bf16[16,2,64,1024]{3,2,1,0:T(8,128)(2,1)} async-done(((bf16[1,2,64,1024]{3,2,1,0:T(8,128)(2,1)}), bf16[16,2,64,1024]{3,2,1,0:T(8,128)(2,1)}) %all-gather.4.cloned.1.call-update) | async-done | bytes 4194320 | tf_op jit(solution)/shard_map/all_gather | solution.py:129
  192.3 101.8 %while.14 = (s32[]{:T(128)}, f32[2,2,64,1024]{3,2,1,0:T(8,128)S(1)}, bf16[16,2,64,1024]{3,2,1,0:T(8,128)(2,1)}, s32[2]{0:T(128)S(1)}, bf16[16,2,64,1024]{3,2,1,0...) while((s32[]{:T(128)}, ...), condition=%wide.region_1.4_spmd, body=%wide.region_0.3_spmd.sunk | while | flops 3023392 | bytes 18367192 | solution.py:84
  194.7 1.2 compare_and_fusion.4
  201.1 1.2 compare_and_fusion.4
  207.4 1.2 compare_and_fusion.4
  213.8 1.2 compare_and_fusion.4
  220.2 1.2 compare_and_fusion.4
  226.5 1.2 compare_and_fusion.4
  232.9 1.2 compare_and_fusion.4
  239.3 1.2 compare_and_fusion.4
  245.6 1.2 compare_and_fusion.4
  252.0 1.2 compare_and_fusion.4
  264.7 1.2 compare_and_fusion.4
  (373 shorter events, 95.9 us)
Async XLA Ops:
  6.5 14.2 %copy-start.1 = (f32[2,1024]{1,0:T(2,128)S(1)}, f32[2,1024]{1,0:T(2,128)}, u32[]{:S(2)}) copy-start(f32[2,1024]{1,0:T(2,128)} %param.19) | copy-start | bytes 24580
  6.5 14.3 %copy-start.2 = (s32[1,1024]{1,0:T(1,128)S(1)}, s32[1,1024]{1,0:T(1,128)}, u32[]{:S(2)}) copy-start(s32[1,1024]{1,0:T(1,128)} %param.17) | copy-start | bytes 12292
  6.5 14.4 %copy-start.3 = (s32[1,1024]{1,0:T(1,128)S(1)}, s32[1,1024]{1,0:T(1,128)}, u32[]{:S(2)}) copy-start(s32[1,1024]{1,0:T(1,128)} %param.16) | copy-start | bytes 12292
  9.0 61.6 %all-to-all-start = ((bf16[16,64,1024]{2,1,0:T(8,128)(2,1)}), bf16[16,64,1024]{2,1,0:T(8,128)(2,1)}, u32[]{:S(2)}, u32[]{:S(2)}) async-start(bf16[16,64,1024]{2,1,0:T(8,128)(2,1)} %stack.34), calls=%async_computation | async-start | bytes 4194304 | tf_op jit(solution)/shard_map/all_to_all | solution.py:99
  20.7 129.4 %all-gather.6.cloned.1.call-start = ((), (), s32[]{:S(2)}) async-start(), calls=%async_computation.3 | async-start | bytes 4456448 | tf_op jit(solution)/shard_map/all_gather | solution.py:128
  92.8 17.4 %copy-start.4 = (s32[16]{0:T(128)S(1)}, s32[16]{0:T(128)}, u32[]{:S(2)}) copy-start(s32[16]{0:T(128)} %param.20) | copy-start | bytes 196
  111.8 21.9 %copy-start.5 = (s32[32]{0:T(128)S(1)}, s32[32]{0:T(128)}, u32[]{:S(2)}) copy-start(s32[32]{0:T(128)} %param.21) | copy-start | bytes 388
  113.1 17.9 %all-to-all-start.1 = ((bf16[1,2,1,16,4096]{4,1,2,0,3:T(2,128)(2,1)}), bf16[1,2,1,16,4096]{4,1,2,0,3:T(2,128)(2,1)S(1)}, u32[]{:S(2)}, u32[]{:S(2)}) async-start(bf16[1,2,1,16,4096]{4,1,2,0,3:T(2,128)(2,1)} %bitcast.29), calls=%async_computation.1 | async-start | bytes 524288 | tf_op jit(solution)/shard_map/all_to_all | solution.py:124
  118.8 73.4 %all-gather.4.cloned.1.call-start = ((), (), s32[]{:S(2)}) async-start(), calls=%async_computation.2 | async-start | bytes 4456448 | tf_op jit(solution)/shard_map/all_gather | solution.py:129
  294.1 1.0 copy-start
Sparse Core Ops, SparseCore 0:
  110.3 39.6 all-gather.5
  151.9 40.2 all-gather.3
